TPU v7x, 32 devices: a whole 2x2x4 slice. The times are simulated.
32 devices in a mesh: db: 8 (over z, x), pb: 4 (over y, core).
Axes of the slice: x: 2, y: 2, z: 4, core: 2. Of those that a mesh axis runs over, the one named last changes fastest.
Arguments:
- queries: bfloat16 [256, 4096], P('pb'), may hold values from -6 to 6
- database: bfloat16 [8192, 4096], P(('db', 'pb')), may hold values from -6 to 6
- slopes: int32 [5], replicated, may hold values from 1 to 6, as said below
Outputs:
- match_score: float32 [256, 8192], P(None, ('db', 'pb'))
Inputs may be any that keep to these rules, and one draw needn't show every extreme that they name: `slopes`: every slope lies in 1 to 6; one of them is 6 and one is 1.
All inputs are finite; a program needn't handle non-finite values.
Results may differ from a plain program's by a relative error of at most 0.0003.
Values may be sent and summed in bfloat16 or wider, within the bound.
A program may use at most 64 MiB of HBM per device.

v0:
```python
import jax
import jax.numpy as jnp
from jax import lax
from jax.sharding import PartitionSpec as P

SEQ = 20
RADIUS = 5
SLOPES = 5
SMAX = 6


variance_floor = 0.25


def padded_2(value, sides, width):
    for axis, dim in sides:
        count, length = (lax.axis_size(axis), value.shape[dim])
        up = [(i, (i + 1) % count) for i in range(count - 1)]
        down = [(j, i) for i, j in up]
        last = lax.slice_in_dim(value, length - width, length, axis=dim)
        leading = lax.slice_in_dim(value, 0, width, axis=dim)
        before = lax.ppermute(last, axis, up)
        after = lax.ppermute(leading, axis, down)
        value = jnp.concatenate([before, value, after], axis=dim)
    return value


def from_behind(value, axis, steps):
    count = lax.axis_size(axis)
    leading, last = (max(0, -steps), min(count, count - steps))
    return lax.ppermute(value, axis, [(source, source + steps) for source in range(leading, last)])


def band_mask(first_frame, frame_count, band_total):
    frame_ids = first_frame + jnp.arange(frame_count, dtype=jnp.int32)
    inside = jnp.logical_and(frame_ids >= 0, frame_ids < band_total)
    return inside.astype(jnp.float32)[None, :]


def contrast(extended, validity):
    out_width = extended.shape[1] - 2 * RADIUS
    masked = extended * validity
    squared = masked * masked
    first_sum = masked[:, :out_width]
    second_sum = squared[:, :out_width]
    counted = validity[:, :out_width]
    for offset in range(1, 2 * RADIUS + 1):
        first_sum = first_sum + masked[:, offset : offset + out_width]
        second_sum = second_sum + squared[:, offset : offset + out_width]
        counted = counted + validity[:, offset : offset + out_width]
    counted = jnp.maximum(counted, 1.0)
    average = first_sum / counted
    spread = second_sum / counted - average * average
    center = extended[:, RADIUS : RADIUS + out_width]
    keeper = validity[:, RADIUS : RADIUS + out_width]
    return keeper * (center - average) / jnp.sqrt(jnp.maximum(spread, variance_floor))


def lagged(field, steps, slope):
    col_pad = steps * SMAX
    padded = jnp.pad(field, ((steps, 0), (col_pad, 0)))
    begin = col_pad - steps * slope
    return lax.dynamic_slice(padded, (jnp.int32(0), begin), field.shape)


def window_sum(field, slope):
    powers = [field]
    stride = 1
    while 2 * stride <= SEQ:
        powers.append(powers[-1] + lagged(powers[-1], stride, slope))
        stride = stride * 2
    summed = None
    filled = 0
    for level in reversed(range(len(powers))):
        if SEQ >> level & 1:
            segment = powers[level] if filled == 0 else lagged(powers[level], filled, slope)
            summed = segment if summed is None else summed + segment
            filled = filled + (1 << level)
    return summed


def best_match(joined, slopes, reach):
    highest = None
    for member in range(SLOPES):
        summed = window_sum(joined, slopes[member])[:, reach:]
        highest = summed if highest is None else jnp.maximum(highest, summed)
    return highest * SEQ ** (-0.5)


def on_device(queries, database, slopes):
    frames = database.shape[0]
    scale = database.shape[1] ** (-0.5)
    reach = SMAX * (SEQ - 1)
    band_total = frames * lax.axis_size(("db", "pb"))
    similarity = (
        lax.dot_general(
            lax.all_gather(queries, "pb", axis=0, tiled=True),
            database,
            (((1,), (1,)), ((), ())),
            preferred_element_type=jnp.float32,
        )
        * scale
    )
    anchor = lax.axis_index(("db", "pb")) * frames
    extended = padded_2(similarity, ((("db", "pb"), 1),), RADIUS)
    normed = contrast(extended, band_mask(anchor - RADIUS, frames + 2 * RADIUS, band_total))
    carried = from_behind(normed[:, frames - reach :], ("db", "pb"), 1)
    joined = jnp.concatenate([carried, normed], axis=1)
    return best_match(joined, slopes, reach)


def solution(mesh):
    placed = (P("pb", None), P(("db", "pb"), None), P())
    return jax.shard_map(
        on_device, mesh=mesh, in_specs=placed, out_specs=P(None, ("db", "pb")), check_vma=False
    )
```

profile of v0, /device:TPU:7, one launch (start us, length us, event | category | flops | bytes accessed | tf_op | source)
XLA Modules:
  0.0 78.4 jit_solution(4593972485175373865)
XLA Ops:
  6.5 0.0 copy-start
  6.5 0.0 all-gather.2.cloned.1.call-start
  6.5 0.7 all-gather.2.cloned.1.call-update
  7.3 0.1 fusion.44
  7.4 24.8 %all-gather.2.cloned.1.call-done = bf16[256,4096]{1,0:T(8,128)(2,1)} async-done(((bf16[64,4096]{1,0:T(8,128)(2,1)}), bf16[256,4096]{1,0:T(8,128)(2,1)}) %all-gather.2.cloned.1.call-update) | async-done | bytes 2097168 | tf_op jit(solution)/shard_map/all_gather | solution.py:97
  32.2 0.0 copy-done
  32.2 2.3 %convolution_multiply_fusion = f32[256,256]{0,1:T(8,128)S(1)} fusion(bf16[256,4096]{1,0:T(8,128)(2,1)} %all-gather.2.cloned.1.call-done, bf16[256,4096]{1,0:T(8,128)(2,1)S(1)} %copy-done), kind=kOutput, calls=%fused_computation | convolution fusion | flops 536936448 | bytes 4456448 | tf_op jit(solution)/shard_map/dot_general | solution.py:96
  34.6 4.2 %collective-permute-start = (f32[256,5]{0,1:T(8,128)S(1)}, f32[256,5]{0,1:T(8,128)S(1)}, u32[]{:S(2)}, u32[]{:S(2)}) collective-permute-start(f32[256,5]{0,1:T(8,128)S(1)} %get-tuple-element.12), channel_id=1, source_target_pairs={{0,1},{1,2},{2,3},{3,4},{4,5},{5,6},{6,7},{7,8},{8,9},{9,10},{10,1... | collective-permute-start | bytes 15368 | tf_op jit(solution)/shard_map/ppermute | solution.py:22
  38.7 1.9 %collective-permute-start.1 = (f32[256,5]{0,1:T(8,128)S(1)}, f32[256,5]{0,1:T(8,128)S(1)}, u32[]{:S(2)}, u32[]{:S(2)}) collective-permute-start(f32[256,5]{0,1:T(8,128)S(1)} %get-tuple-element.13), channel_id=1, source_target_pairs={{1,0},{2,1},{3,2},{4,3},{5,4},{6,5},{7,6},{8,7},{9,8},{10,9},{11,1... | collective-permute-start | bytes 15368 | tf_op jit(solution)/shard_map/ppermute | solution.py:23
  40.7 0.0 collective-permute-done
  40.7 4.8 %collective-permute-done.1 = f32[256,5]{0,1:T(8,128)S(1)} collective-permute-done((f32[256,5]{0,1:T(8,128)S(1)}, f32[256,5]{0,1:T(8,128)S(1)}, u32[]{:S(2)}, u32[]{:S(2)}) %collective-permute-start.1) | collective-permute-done | bytes 5152 | tf_op jit(solution)/shard_map/ppermute | solution.py:23
  45.5 0.1 fusion.42
  45.6 0.0 copy-start.1
  45.6 0.5 fusion.34
  46.2 1.9 %collective-permute-start.2 = (f32[256,114]{0,1:T(8,128)S(1)}, f32[256,114]{0,1:T(8,128)S(1)}, u32[]{:S(2)}, u32[]{:S(2)}) collective-permute-start(f32[256,114]{0,1:T(8,128)S(1)} %slice.220), channel_id=1, source_target_pairs={{0,1},{1,2},{2,3},{3,4},{4,5},{5,6},{6,7},{7,8},{8,9},{9,10},{10,1... | collective-permute-start | bytes 350216 | tf_op jit(solution)/shard_map/ppermute | solution.py:31
  48.1 0.0 copy-done.1
  48.2 0.7 fusion.45
  67.1 0.0 collective-permute-done.2
  67.1 0.7 fusion.14
  67.8 0.2 fusion.4
  68.0 0.2 fusion.9
  68.2 0.3 fusion.2
  68.5 0.2 fusion.7
  68.7 0.2 fusion.8
  68.9 0.3 fusion
  69.2 0.2 fusion.5
  69.4 0.2 fusion.6
  69.6 1.2 %fusion.21 = f32[256,256]{0,1:T(8,128)S(1)} fusion(s32[]{:T(128)S(6)} %add.489, f32[256,370]{0,1:T(8,128)S(1)} %fusion.5, s32[]{:T(128)S(6)} %add.491, f32[256,370]{0,1:T(8,128)S(1)} %fusion.6, s32[]{:T(128)S(6)} %add.493, f32[256,370]{0,1:T(8,128)S(1)} %fusion.7, s32[]{:T(128)S(6)} %add.495, f32[256,370]{0,1:T(8,128)S(1)} %fusion.8, s32[]{:T(128)S(6)} %add.497, ...), kind=kLoop, calls=%fused_computation.49 | loop fusion | flops 983040 | bytes 5423144 | tf_op jit(solution)/shard_map/mul | solution.py:87
  70.8 0.8 %copy.4 = f32[256,256]{1,0:T(8,128)} copy(f32[256,256]{0,1:T(8,128)S(1)} %fusion.21) | data formatting | bytes 524288 | tf_op jit(solution)/shard_map/mul | solution.py:87
  (5 shorter events, 0.1 us)
Async XLA Ops:
  6.5 25.7 %copy-start = (bf16[256,4096]{1,0:T(8,128)(2,1)S(1)}, bf16[256,4096]{1,0:T(8,128)(2,1)}, u32[]{:S(2)}) copy-start(bf16[256,4096]{1,0:T(8,128)(2,1)} %param.4) | copy-start | bytes 6291460
  6.5 25.7 %all-gather.2.cloned.1.call-start = ((), (), s32[]{:S(2)}) async-start(), calls=%async_computation | async-start | bytes 2621440 | tf_op jit(solution)/shard_map/all_gather | solution.py:97
  34.6 6.1 %collective-permute-start = (f32[256,5]{0,1:T(8,128)S(1)}, f32[256,5]{0,1:T(8,128)S(1)}, u32[]{:S(2)}, u32[]{:S(2)}) collective-permute-start(f32[256,5]{0,1:T(8,128)S(1)} %get-tuple-element.12), channel_id=1, source_target_pairs={{0,1},{1,2},{2,3},{3,4},{4,5},{5,6},{6,7},{7,8},{8,9},{9,10},{10,1... | collective-permute-start | bytes 15368 | tf_op jit(solution)/shard_map/ppermute | solution.py:22
  38.7 6.8 %collective-permute-start.1 = (f32[256,5]{0,1:T(8,128)S(1)}, f32[256,5]{0,1:T(8,128)S(1)}, u32[]{:S(2)}, u32[]{:S(2)}) collective-permute-start(f32[256,5]{0,1:T(8,128)S(1)} %get-tuple-element.13), channel_id=1, source_target_pairs={{1,0},{2,1},{3,2},{4,3},{5,4},{6,5},{7,6},{8,7},{9,8},{10,9},{11,1... | collective-permute-start | bytes 15368 | tf_op jit(solution)/shard_map/ppermute | solution.py:23
  45.6 2.5 %copy-start.1 = (s32[5]{0:T(128)S(1)}, s32[5]{0:T(128)}, u32[]{:S(2)}) copy-start(s32[5]{0:T(128)} %param.5) | copy-start | bytes 64
  46.2 20.9 %collective-permute-start.2 = (f32[256,114]{0,1:T(8,128)S(1)}, f32[256,114]{0,1:T(8,128)S(1)}, u32[]{:S(2)}, u32[]{:S(2)}) collective-permute-start(f32[256,114]{0,1:T(8,128)S(1)} %slice.220), channel_id=1, source_target_pairs={{0,1},{1,2},{2,3},{3,4},{4,5},{5,6},{6,7},{7,8},{8,9},{9,10},{10,1... | collective-permute-start | bytes 350216 | tf_op jit(solution)/shard_map/ppermute | solution.py:31
Sparse Core Ops, SparseCore 0:
  8.9 23.2 all-gather.1
where the time goes:
time: 78.9 us; the launch traced here: 78.4 us
  between operations  31.8 us (40%)
  waiting for transfers between devices  30.4 us (39%)
  starting transfers between devices  8.05 us (10%)
  other arithmetic  4.35 us (6%)
  matrix products  2.33 us (3%)
  local copies, waits for them, and re-layouts  1.52 us (2%)
    all_gather x1, waiting for transfers between devices, on_device(): lax.all_gather(queries, 'pb', axis=0, tiled=True)  24.8 us
    ppermute x1, waiting for transfers between devices, padded_2(): after = lax.ppermute(leading, axis, down)  4.81 us
    ppermute x1, starting transfers between devices, padded_2(): before = lax.ppermute(last, axis, up)  4.18 us
    add x9, other arithmetic, window_sum(): powers.append(powers[-1] + lagged(powers[-1], stride, slope))  2.42 us
    dot_general x1, matrix products, on_device(): lax.dot_general(lax.all_gather(queries, 'pb', axis=0, tiled=True), databa...  2.33 us
    ppermute x1, starting transfers between devices, from_behind(): lax.ppermute(value, axis, [(source, source + steps) for source in range(l...  1.94 us
    ppermute x1, starting transfers between devices, padded_2(): after = lax.ppermute(leading, axis, down)  1.92 us
  transfers between devices with their start and end apart: 4, of which 2 were waited for; matrix products, arithmetic and copies ran while one was open for 1% of the time, Pallas kernels for 0%

commit v1 on v0

v1 whole, which is shorter than its diff:
```python
import functools

import jax
import jax.numpy as jnp
from jax import lax
from jax.experimental import pallas as pl
from jax.experimental.pallas import tpu as pltpu
from jax.sharding import PartitionSpec as P

SEQ = 20
RADIUS = 5
SLOPES = 5
SMAX = 6
CHUNKS = 4
LEFT = 128
RIGHT = 8
LANES = 128

variance_floor = 0.25
MESH = pl.DeviceIdType.MESH


def similarity_kernel(
    n_db, n_pb, q_ref, base_ref, out_ref, qbuf, base, left_in, right_in,
    load_sem, own_sem, far_send, far_recv, core_send, core_recv, fwd_send, fwd_recv, edge_send, edge_recv,
):
    db, pb = lax.axis_index("db"), lax.axis_index("pb")
    rows, depth = q_ref.shape
    frames = base_ref.shape[0]
    groups = n_pb // 2
    core, group = lax.rem(pb, 2), pb // 2
    mate = pb + 1 - 2 * core
    me = db * n_pb + pb
    total = n_db * n_pb
    far = [lax.rem(group + step, groups) * 2 + core for step in range(1, groups)]
    source = [lax.rem(group + groups - step, groups) * 2 + core for step in range(1, groups)]
    width = depth // CHUNKS
    has_left, has_right = me > 0, me < total - 1
    left, right = me - 1, me + 1

    load = pltpu.make_async_copy(base_ref, base, load_sem)
    load.start()
    own = pltpu.make_async_copy(q_ref, qbuf.at[pl.ds(pb * rows, rows), :], own_sem)
    own.start()

    barrier = pltpu.get_barrier_semaphore()
    for peer in [mate] + far:
        pl.semaphore_signal(barrier, inc=1, device_id={"db": db, "pb": peer}, device_id_type=MESH)

    @pl.when(has_left)
    def _():
        pl.semaphore_signal(barrier, inc=1, device_id={"db": left // n_pb, "pb": lax.rem(left, n_pb)}, device_id_type=MESH)

    @pl.when(has_right)
    def _():
        pl.semaphore_signal(barrier, inc=1, device_id={"db": right // n_pb, "pb": lax.rem(right, n_pb)}, device_id_type=MESH)

    pl.semaphore_wait(barrier, groups + has_left.astype(jnp.int32) + has_right.astype(jnp.int32))

    def piece(owner, chunk):
        return qbuf.at[pl.ds(owner * rows, rows), pl.ds(chunk * width, width)]

    sent = []
    for chunk in range(CHUNKS):
        for step, peer in enumerate(far):
            copy = pltpu.make_async_remote_copy(
                src_ref=q_ref.at[:, pl.ds(chunk * width, width)],
                dst_ref=piece(pb, chunk),
                send_sem=far_send.at[step, chunk],
                recv_sem=far_recv.at[step, chunk],
                device_id={"db": db, "pb": peer},
                device_id_type=MESH,
            )
            copy.start()
            sent.append(copy)
    near = pltpu.make_async_remote_copy(
        src_ref=q_ref,
        dst_ref=qbuf.at[pl.ds(pb * rows, rows), :],
        send_sem=core_send,
        recv_sem=core_recv,
        device_id={"db": db, "pb": mate},
        device_id_type=MESH,
    )
    near.start()
    load.wait()
    own.wait()
    near.wait()

    passed = [[] for _ in range(CHUNKS)]
    for chunk in range(CHUNKS):
        for step in range(groups - 1):
            pltpu.make_async_remote_copy(
                src_ref=piece(source[step], chunk),
                dst_ref=piece(source[step], chunk),
                send_sem=far_send.at[step, chunk],
                recv_sem=far_recv.at[step, chunk],
                device_id={"db": db, "pb": mate},
                device_id_type=MESH,
            ).wait_recv()
            copy = pltpu.make_async_remote_copy(
                src_ref=piece(source[step], chunk),
                dst_ref=piece(source[step], chunk),
                send_sem=fwd_send.at[step, chunk],
                recv_sem=fwd_recv.at[step, chunk],
                device_id={"db": db, "pb": mate},
                device_id_type=MESH,
            )
            copy.start()
            passed[chunk].append(copy)
        for copy in passed[chunk]:
            copy.wait_recv()
        cols = pl.ds(chunk * width, width)
        term = lax.dot_general(
            base[:, cols], qbuf[:, cols], (((1,), (1,)), ((), ())), preferred_element_type=jnp.float32
        )
        if chunk == 0:
            out_ref[pl.ds(LEFT, frames), :] = term
        elif chunk < CHUNKS - 1:
            out_ref[pl.ds(LEFT, frames), :] += term
        else:
            out_ref[pl.ds(LEFT, frames), :] = (out_ref[pl.ds(LEFT, frames), :] + term) * depth ** (-0.5)

    ahead = pltpu.make_async_remote_copy(
        src_ref=out_ref.at[pl.ds(frames, LEFT), :],
        dst_ref=left_in,
        send_sem=edge_send.at[0],
        recv_sem=edge_recv.at[0],
        device_id={"db": lax.rem(right // n_pb, n_db), "pb": lax.rem(right, n_pb)},
        device_id_type=MESH,
    )
    behind = pltpu.make_async_remote_copy(
        src_ref=out_ref.at[pl.ds(LEFT, RIGHT), :],
        dst_ref=right_in,
        send_sem=edge_send.at[1],
        recv_sem=edge_recv.at[1],
        device_id={"db": jnp.maximum(left, 0) // n_pb, "pb": lax.rem(jnp.maximum(left, 0), n_pb)},
        device_id_type=MESH,
    )

    @pl.when(has_right)
    def _():
        ahead.start()

    @pl.when(has_left)
    def _():
        behind.start()

    for copy in sent:
        copy.wait_send()
    for copies in passed:
        for copy in copies:
            copy.wait_send()

    @pl.when(has_left)
    def _():
        ahead.wait_recv()
        out_ref[pl.ds(0, LEFT), :] = left_in[...]
        behind.wait_send()

    @pl.when(me == 0)
    def _():
        out_ref[pl.ds(0, LEFT), :] = jnp.zeros((LEFT, out_ref.shape[1]), jnp.float32)

    @pl.when(has_right)
    def _():
        behind.wait_recv()
        out_ref[pl.ds(LEFT + frames, RIGHT), :] = right_in[...]
        ahead.wait_send()

    @pl.when(me == total - 1)
    def _():
        out_ref[pl.ds(LEFT + frames, RIGHT), :] = jnp.zeros((RIGHT, out_ref.shape[1]), jnp.float32)


def similarities(queries, database, n_db, n_pb):
    rows, depth = queries.shape
    frames = database.shape[0]
    nq = rows * n_pb
    groups = n_pb // 2
    far = (max(groups - 1, 1), CHUNKS)
    return pl.pallas_call(
        functools.partial(similarity_kernel, n_db, n_pb),
        out_shape=jax.ShapeDtypeStruct((LEFT + frames + RIGHT, nq), jnp.float32),
        in_specs=[pl.BlockSpec(memory_space=pl.ANY)] * 2,
        out_specs=pl.BlockSpec(memory_space=pltpu.VMEM),
        scratch_shapes=[
            pltpu.VMEM((nq, depth), jnp.bfloat16),
            pltpu.VMEM((frames, depth), jnp.bfloat16),
            pltpu.VMEM((LEFT, nq), jnp.float32),
            pltpu.VMEM((RIGHT, nq), jnp.float32),
            pltpu.SemaphoreType.DMA,
            pltpu.SemaphoreType.DMA,
            pltpu.SemaphoreType.DMA(far),
            pltpu.SemaphoreType.DMA(far),
            pltpu.SemaphoreType.DMA,
            pltpu.SemaphoreType.DMA,
            pltpu.SemaphoreType.DMA(far),
            pltpu.SemaphoreType.DMA(far),
            pltpu.SemaphoreType.DMA((2,)),
            pltpu.SemaphoreType.DMA((2,)),
        ],
        compiler_params=pltpu.CompilerParams(
            collective_id=0, has_side_effects=True, vmem_limit_bytes=48 * 1024 * 1024
        ),
    )(queries, database)


def score_kernel(band_total, n_pb, slopes_ref, sim_ref, out_ref, field, normed, two, four, eight, best):
    span, nq = sim_ref.shape
    frames = out_ref.shape[1]
    pieces = nq // LANES
    anchor = (lax.axis_index("db") * n_pb + lax.axis_index("pb")) * frames - LEFT

    ids = lax.broadcasted_iota(jnp.int32, (span, LANES), 0) + anchor
    inside = jnp.logical_and(ids >= 0, ids < band_total)
    for p in range(pieces):
        field[p] = jnp.where(inside, sim_ref[:, p * LANES : (p + 1) * LANES], 0.0)

    first, count = 8, span - 16
    center_ids = lax.broadcasted_iota(jnp.int32, (count, LANES), 0) + (anchor + first)
    counted = jnp.minimum(center_ids + RADIUS, band_total - 1) - jnp.maximum(center_ids - RADIUS, 0) + 1
    share = 1.0 / jnp.maximum(counted, 1).astype(jnp.float32)
    keep = jnp.logical_and(center_ids >= 0, center_ids < band_total)
    for p in range(pieces):
        first_sum = None
        for offset in range(-RADIUS, RADIUS + 1):
            part = field[p, pl.ds(first + offset, count), :]
            square = part * part
            first_sum = part if first_sum is None else first_sum + part
            second_sum = square if offset == -RADIUS else second_sum + square
        average = first_sum * share
        spread = second_sum * share - average * average
        center = field[p, pl.ds(first, count), :]
        value = (center - average) * lax.rsqrt(jnp.maximum(spread, variance_floor))
        normed[p, pl.ds(first, count), :] = jnp.where(keep, value, 0.0)

    def lagged(source, p, lo, steps, slope, lane):
        rows = span - RIGHT - lo
        begin = lo - steps * slope
        shifted = pltpu.roll(source[p, pl.ds(begin, rows), :], steps, 1)
        if p == 0:
            return jnp.where(lane[:rows] < steps, 0.0, shifted)
        earlier = pltpu.roll(source[p - 1, pl.ds(begin, rows), :], steps, 1)
        return jnp.where(lane[:rows] < steps, earlier, shifted)

    lane = lax.broadcasted_iota(jnp.int32, (span, LANES), 1)

    def member(index, carry):
        slope = slopes_ref[index]
        for source, target, lo, steps in (
            (normed, two, 16, 1),
            (two, four, 32, 2),
            (four, eight, 80, 4),
        ):
            for p in range(pieces):
                target[p, pl.ds(lo, span - RIGHT - lo), :] = source[p, pl.ds(lo, span - RIGHT - lo), :] + lagged(
                    source, p, lo, steps, slope, lane
                )
        for p in range(pieces):
            summed = eight[p, pl.ds(LEFT, frames), :] + lagged(eight, p, LEFT, 8, slope, lane)
            summed = summed + lagged(four, p, LEFT, 16, slope, lane)
            best[p] = jnp.maximum(best[p], summed)
        return carry

    best[...] = jnp.full(best.shape, -jnp.inf, jnp.float32)
    lax.fori_loop(0, slopes_ref.shape[0], member, 0)
    for p in range(pieces):
        out_ref[p * LANES : (p + 1) * LANES, :] = best[p].T * SEQ ** (-0.5)


def scores(similarity, slopes, band_total, n_pb):
    span, nq = similarity.shape
    frames = span - LEFT - RIGHT
    pieces = nq // LANES
    return pl.pallas_call(
        functools.partial(score_kernel, band_total, n_pb),
        out_shape=jax.ShapeDtypeStruct((nq, frames), jnp.float32),
        in_specs=[pl.BlockSpec(memory_space=pltpu.SMEM), pl.BlockSpec(memory_space=pltpu.VMEM)],
        out_specs=pl.BlockSpec(memory_space=pltpu.VMEM),
        scratch_shapes=[pltpu.VMEM((pieces, span, LANES), jnp.float32)] * 5
        + [pltpu.VMEM((pieces, frames, LANES), jnp.float32)],
        compiler_params=pltpu.CompilerParams(vmem_limit_bytes=48 * 1024 * 1024),
    )(slopes, similarity)


def on_device(n_db, n_pb, queries, database, slopes):
    similarity = similarities(queries, database, n_db, n_pb)
    return scores(similarity, slopes, database.shape[0] * n_db * n_pb, n_pb)


def solution(mesh):
    placed = (P("pb", None), P(("db", "pb"), None), P())
    sizes = (mesh.shape["db"], mesh.shape["pb"])
    return jax.shard_map(
        functools.partial(on_device, *sizes),
        mesh=mesh,
        in_specs=placed,
        out_specs=P(None, ("db", "pb")),
        check_vma=False,
    )
```

time: 78.9 us -> 30.8 us (0.39)
  the two profiles are of different devices: /device:TPU:7 before, /device:TPU:8 now
where the time goes in v1:
time: 30.8 us; the launch traced here: 30.6 us
  Pallas kernels  28 us (91%)
  local copies, waits for them, and re-layouts  2.64 us (9%)
    pallas_call x1, Pallas kernels, similarities(): pl.pallas_call(functools.partial(similarity_kernel, n_db, n_pb), out_shap...  21.1 us
    pallas_call x1, Pallas kernels, scores(): pl.pallas_call(functools.partial(score_kernel, band_total, n_pb), out_sha...  6.91 us
    unnamed x6, local copies, waits for them, and re-layouts  2.64 us

profile of v1, /device:TPU:8, one launch (start us, length us, event | category | flops | bytes accessed | tf_op | source)
XLA Modules:
  0.0 30.6 jit_solution(6659714769898505292)
XLA Ops:
  0.0 0.0 copy-start
  0.0 1.6 %copy-done = bf16[256,4096]{1,0:T(8,128)(2,1)S(1)} copy-done((bf16[256,4096]{1,0:T(8,128)(2,1)S(1)}, bf16[256,4096]{1,0:T(8,128)(2,1)}, u32[]{:S(2)}) %copy-start) | copy-done | bytes 2097176
  1.6 0.0 copy-start.1
  1.6 1.0 %copy-done.1 = bf16[64,4096]{1,0:T(8,128)(2,1)S(1)} copy-done((bf16[64,4096]{1,0:T(8,128)(2,1)S(1)}, bf16[64,4096]{1,0:T(8,128)(2,1)}, u32[]{:S(2)}) %copy-start.1) | copy-done | bytes 524312
  2.6 0.0 copy-start.2
  2.6 21.1 %shard_map.37.sim_ref = f32[392,256]{1,0:T(8,128)S(1)} custom-call(bf16[64,4096]{1,0:T(8,128)(2,1)S(1)} %copy-done.1, bf16[256,4096]{1,0:T(8,128)(2,1)S(1)} %copy-done), custom_call_target="tpu_custom_call" | custom-call | tf_op jit(solution)/shard_map/pallas_call | solution.py:181
  23.7 0.0 copy-done.2
  23.7 6.9 %shard_map.38 = f32[256,256]{1,0:T(8,128)} custom-call(s32[5]{0:T(128)S(1)} %copy-done.2, f32[392,256]{1,0:T(8,128)S(1)} %shard_map.37.sim_ref), custom_call_target="tpu_custom_call" | custom-call | tf_op jit(solution)/shard_map/pallas_call | solution.py:275
Async XLA Ops:
  0.0 1.6 %copy-start = (bf16[256,4096]{1,0:T(8,128)(2,1)S(1)}, bf16[256,4096]{1,0:T(8,128)(2,1)}, u32[]{:S(2)}) copy-start(bf16[256,4096]{1,0:T(8,128)(2,1)} %base_ref.1) | copy-start | bytes 6291460
  1.6 1.0 %copy-start.1 = (bf16[64,4096]{1,0:T(8,128)(2,1)S(1)}, bf16[64,4096]{1,0:T(8,128)(2,1)}, u32[]{:S(2)}) copy-start(bf16[64,4096]{1,0:T(8,128)(2,1)} %q_ref.1) | copy-start | bytes 1572868
  2.6 21.1 %copy-start.2 = (s32[5]{0:T(128)S(1)}, s32[5]{0:T(128)}, u32[]{:S(2)}) copy-start(s32[5]{0:T(128)} %slopes_ref.1) | copy-start | bytes 64

commit v2 on v1

--- a/solution.py
+++ b/solution.py
@@ -181,7 +181,7 @@
     return pl.pallas_call(
         functools.partial(similarity_kernel, n_db, n_pb),
         out_shape=jax.ShapeDtypeStruct((LEFT + frames + RIGHT, nq), jnp.float32),
-        in_specs=[pl.BlockSpec(memory_space=pl.ANY)] * 2,
+        in_specs=[pl.BlockSpec(memory_space=pltpu.HBM)] * 2,
         out_specs=pl.BlockSpec(memory_space=pltpu.VMEM),
         scratch_shapes=[
             pltpu.VMEM((nq, depth), jnp.bfloat16),
@@ -200,7 +200,7 @@
             pltpu.SemaphoreType.DMA((2,)),
         ],
         compiler_params=pltpu.CompilerParams(
-            collective_id=0, has_side_effects=True, vmem_limit_bytes=48 * 1024 * 1024
+            collective_id=0, has_side_effects=True, vmem_limit_bytes=60 * 1024 * 1024
         ),
     )(queries, database)
 
@@ -234,36 +234,35 @@
         value = (center - average) * lax.rsqrt(jnp.maximum(spread, variance_floor))
         normed[p, pl.ds(first, count), :] = jnp.where(keep, value, 0.0)
 
-    def lagged(source, p, lo, steps, slope, lane):
+    lane = lax.broadcasted_iota(jnp.int32, (1, LANES), 1)
+
+    def lagged(source, lo, steps, slope):
         rows = span - RIGHT - lo
-        begin = lo - steps * slope
-        shifted = pltpu.roll(source[p, pl.ds(begin, rows), :], steps, 1)
-        if p == 0:
-            return jnp.where(lane[:rows] < steps, 0.0, shifted)
-        earlier = pltpu.roll(source[p - 1, pl.ds(begin, rows), :], steps, 1)
-        return jnp.where(lane[:rows] < steps, earlier, shifted)
-
-    lane = lax.broadcasted_iota(jnp.int32, (span, LANES), 1)
-
-    def member(index, carry):
-        slope = slopes_ref[index]
-        for source, target, lo, steps in (
-            (normed, two, 16, 1),
-            (two, four, 32, 2),
-            (four, eight, 80, 4),
-        ):
+        earlier, parts = 0.0, []
+        for p in range(pieces):
+            rolled = pltpu.roll(source[p, pl.ds(lo - steps * slope, rows), :], steps, 1)
+            parts.append(jnp.where(lane < steps, earlier, rolled))
+            earlier = rolled
+        return parts
+
+    best[...] = jnp.full(best.shape, -jnp.inf, jnp.float32)
+    for slope in range(1, SMAX + 1):
+        present = slopes_ref[0] == slope
+        for index in range(1, slopes_ref.shape[0]):
+            present = jnp.logical_or(present, slopes_ref[index] == slope)
+
+        @pl.when(present)
+        def _():
+            for source, target, lo, steps in ((normed, two, 16, 1), (two, four, 32, 2), (four, eight, 80, 4)):
+                parts = lagged(source, lo, steps, slope)
+                for p in range(pieces):
+                    target[p, pl.ds(lo, span - RIGHT - lo), :] = source[p, pl.ds(lo, span - RIGHT - lo), :] + parts[p]
+            upper = lagged(eight, LEFT, 8, slope)
+            tail = lagged(four, LEFT, 16, slope)
             for p in range(pieces):
-                target[p, pl.ds(lo, span - RIGHT - lo), :] = source[p, pl.ds(lo, span - RIGHT - lo), :] + lagged(
-                    source, p, lo, steps, slope, lane
-                )
-        for p in range(pieces):
-            summed = eight[p, pl.ds(LEFT, frames), :] + lagged(eight, p, LEFT, 8, slope, lane)
-            summed = summed + lagged(four, p, LEFT, 16, slope, lane)
-            best[p] = jnp.maximum(best[p], summed)
-        return carry
-
-    best[...] = jnp.full(best.shape, -jnp.inf, jnp.float32)
-    lax.fori_loop(0, slopes_ref.shape[0], member, 0)
+                summed = eight[p, pl.ds(LEFT, frames), :] + upper[p] + tail[p]
+                best[p] = jnp.maximum(best[p], summed)
+
     for p in range(pieces):
         out_ref[p * LANES : (p + 1) * LANES, :] = best[p].T * SEQ ** (-0.5)
 

time: 30.8 us -> 26.7 us (0.87)
  Pallas kernels: 28 us -> 25.3 us
  local copies, waits for them, and re-layouts: 2.64 us -> 1 us
    pallas_call x1, Pallas kernels: 6.91 us -> 3.48 us  [scores(): pl.pallas_call(functools.partial(score_kernel, band_total, n_pb), out_sha...]
    unnamed x6 -> x4, local copies, waits for them, and re-layouts: 2.64 us -> 1 us
    pallas_call x1, Pallas kernels: 21.1 us -> 21.8 us  [similarities(): pl.pallas_call(functools.partial(similarity_kernel, n_db, n_pb), out_shap...]
where the time goes in v2:
time: 26.7 us; the launch traced here: 26.4 us
  Pallas kernels  25.3 us (95%)
  local copies, waits for them, and re-layouts  1 us (4%)
    pallas_call x1, Pallas kernels, similarities(): pl.pallas_call(functools.partial(similarity_kernel, n_db, n_pb), out_shap...  21.8 us
    pallas_call x1, Pallas kernels, scores(): pl.pallas_call(functools.partial(score_kernel, band_total, n_pb), out_sha...  3.48 us
    unnamed x4, local copies, waits for them, and re-layouts  1 us

profile of v2, /device:TPU:8, one launch (start us, length us, event | category | flops | bytes accessed | tf_op | source)
XLA Modules:
  0.0 26.4 jit_solution(12531191046409797071)
XLA Ops:
  0.0 0.0 copy-start.1
  0.0 21.8 %shard_map.37.sim_ref = f32[392,256]{1,0:T(8,128)} custom-call(bf16[64,4096]{1,0:T(8,128)(2,1)} %q_ref.1, bf16[256,4096]{1,0:T(8,128)(2,1)} %base_ref.1), custom_call_target="tpu_custom_call" | custom-call | tf_op jit(solution)/shard_map/pallas_call | solution.py:181
  21.9 0.0 copy-done.1
  21.9 0.0 copy-start
  21.9 1.0 %copy-done = f32[392,256]{1,0:T(8,128)S(1)} copy-done((f32[392,256]{1,0:T(8,128)S(1)}, f32[392,256]{1,0:T(8,128)}, u32[]{:S(2)}) %copy-start) | copy-done | bytes 401432
  22.9 3.5 %shard_map.38 = f32[256,256]{1,0:T(8,128)} custom-call(s32[5]{0:T(128)S(1)} %copy-done.1, f32[392,256]{1,0:T(8,128)S(1)} %copy-done), custom_call_target="tpu_custom_call" | custom-call | tf_op jit(solution)/shard_map/pallas_call | solution.py:274
Async XLA Ops:
  0.0 21.9 %copy-start.1 = (s32[5]{0:T(128)S(1)}, s32[5]{0:T(128)}, u32[]{:S(2)}) copy-start(s32[5]{0:T(128)} %slopes_ref.1) | copy-start | bytes 64
  21.9 1.0 %copy-start = (f32[392,256]{1,0:T(8,128)S(1)}, f32[392,256]{1,0:T(8,128)}, u32[]{:S(2)}) copy-start(f32[392,256]{1,0:T(8,128)} %shard_map.37.sim_ref) | copy-start | bytes 1204228

commit v3 on v2

v3 whole, which is shorter than its diff:
```python
import functools

import jax
import jax.numpy as jnp
from jax import lax
from jax.experimental import pallas as pl
from jax.experimental.pallas import tpu as pltpu
from jax.sharding import PartitionSpec as P

SEQ = 20
RADIUS = 5
SLOPES = 5
SMAX = 6
CHUNKS = 4
LEFT = 128
RIGHT = 8

variance_floor = 0.25
MESH = pl.DeviceIdType.MESH


def similarity_kernel(
    n_db, n_pb, q_ref, base_ref, out_ref, qbuf, base, left_in, right_in,
    load_sem, own_sem, far_send, far_recv, core_send, core_recv, side_send, side_recv,
    fwd_send, fwd_recv, edge_send, edge_recv,
):
    db, pb = lax.axis_index("db"), lax.axis_index("pb")
    rows, depth = q_ref.shape
    frames = base_ref.shape[0]
    groups = n_pb // 2
    core, group = lax.rem(pb, 2), pb // 2
    mate = pb + 1 - 2 * core
    half = lax.rem(db, 2)
    buddy = db + 1 - 2 * half
    me = db * n_pb + pb
    total = n_db * n_pb
    far = [lax.rem(group + step, groups) * 2 + core for step in range(1, groups)]
    origin = [lax.rem(group + groups - step, groups) for step in range(1, groups)]
    width = depth // (2 * CHUNKS)
    has_left, has_right = me > 0, me < total - 1
    left, right = jnp.maximum(me - 1, 0), jnp.minimum(me + 1, total - 1)

    own = pltpu.make_async_copy(q_ref, qbuf.at[group, pl.ds(core * rows, rows), :], own_sem)
    own.start()
    load = pltpu.make_async_copy(base_ref, base, load_sem)
    load.start()

    def device(db, pb):
        return {"db": db, "pb": pb}

    barrier = pltpu.get_barrier_semaphore()
    for peer in [device(db, mate), device(buddy, pb)] + [device(db, peer) for peer in far]:
        pl.semaphore_signal(barrier, inc=1, device_id=peer, device_id_type=MESH)

    @pl.when(has_left)
    def _():
        pl.semaphore_signal(
            barrier, inc=1, device_id=device(left // n_pb, lax.rem(left, n_pb)), device_id_type=MESH
        )

    @pl.when(has_right)
    def _():
        pl.semaphore_signal(
            barrier, inc=1, device_id=device(right // n_pb, lax.rem(right, n_pb)), device_id_type=MESH
        )

    pl.semaphore_wait(barrier, groups + 1 + has_left.astype(jnp.int32) + has_right.astype(jnp.int32))

    def columns(part, chunk):
        return pl.ds(pl.multiple_of(part * (depth // 2) + chunk * width, width), width)

    def piece(block, side, part, chunk):
        return qbuf.at[block, pl.ds(side * rows, rows), columns(part, chunk)]

    def remote(src, dst, send, recv, target):
        return pltpu.make_async_remote_copy(
            src_ref=src, dst_ref=dst, send_sem=send, recv_sem=recv, device_id=target, device_id_type=MESH
        )

    sent = []

    def go(copy):
        copy.start()
        sent.append(copy)

    for chunk in range(CHUNKS):
        for step, peer in enumerate(far):
            go(
                remote(
                    q_ref.at[:, columns(half, chunk)],
                    piece(group, core, half, chunk),
                    far_send.at[step, chunk],
                    far_recv.at[step, chunk],
                    device(db, peer),
                )
            )
    near = remote(
        q_ref, qbuf.at[group, pl.ds(core * rows, rows), :], core_send, core_recv, device(db, mate)
    )
    go(near)
    load.wait()
    own.wait()

    def product(block, cols):
        return lax.dot_general(
            base[:, cols], qbuf[block, :, cols], (((1,), (1,)), ((), ())), preferred_element_type=jnp.float32
        )

    def ahead(block):
        return remote(
            out_ref.at[block, pl.ds(frames, LEFT), :],
            left_in.at[block],
            edge_send.at[0, block],
            edge_recv.at[0, block],
            device(right // n_pb, lax.rem(right, n_pb)),
        )

    def behind(block):
        return remote(
            out_ref.at[block, pl.ds(LEFT, RIGHT), :],
            right_in.at[block],
            edge_send.at[1, block],
            edge_recv.at[1, block],
            device(left // n_pb, lax.rem(left, n_pb)),
        )

    def send_edges(block):
        @pl.when(has_right)
        def _():
            ahead(block).start()

        @pl.when(has_left)
        def _():
            behind(block).start()

    scale = depth ** (-0.5)
    mine = pl.ds(LEFT, frames)

    def first(step, chunk):
        block = piece(origin[step], core, half, chunk)
        remote(block, block, far_send.at[step, chunk], far_recv.at[step, chunk], device(db, mate)).wait_recv()
        go(remote(block, block, side_send.at[step, chunk], side_recv.at[step, chunk], device(buddy, pb)))
        go(remote(block, block, fwd_send.at[0, step, chunk], fwd_recv.at[0, step, chunk], device(db, mate)))

    def second(step, chunk):
        block = piece(origin[step], core, 1 - half, chunk)
        remote(block, block, side_send.at[step, chunk], side_recv.at[step, chunk], device(db, mate)).wait_recv()
        go(remote(block, block, fwd_send.at[1, step, chunk], fwd_recv.at[1, step, chunk], device(db, mate)))

    def multiply(order, step, chunk):
        part = half if order == 0 else 1 - half
        block = piece(origin[step], 1 - core, part, chunk)
        remote(
            block, block, fwd_send.at[order, step, chunk], fwd_recv.at[order, step, chunk], device(db, mate)
        ).wait_recv()
        term = product(origin[step], columns(part, chunk))
        if order == 0 and chunk == 0:
            out_ref[origin[step], mine, :] = term
        elif order == 1 and chunk == CHUNKS - 1:
            out_ref[origin[step], mine, :] = (out_ref[origin[step], mine, :] + term) * scale
        else:
            out_ref[origin[step], mine, :] += term

    far_steps = range(groups - 1)
    for stage in range(CHUNKS + 2):
        for step in far_steps:
            if stage < CHUNKS:
                first(step, stage)
            if 1 <= stage <= CHUNKS:
                second(step, stage - 1)
        if stage == 0:
            near.wait_recv()
            out_ref[group, mine, :] = product(group, slice(None)) * scale
            send_edges(group)
        for step in far_steps:
            if 1 <= stage <= CHUNKS:
                multiply(0, step, stage - 1)
            if stage >= 2:
                multiply(1, step, stage - 2)
    for step in far_steps:
        send_edges(origin[step])

    for copy in sent:
        copy.wait_send()

    @pl.when(has_left)
    def _():
        for block in range(groups):
            ahead(block).wait_recv()
            out_ref[block, pl.ds(0, LEFT), :] = left_in[block]
            behind(block).wait_send()

    @pl.when(me == 0)
    def _():
        out_ref[:, pl.ds(0, LEFT), :] = jnp.zeros(left_in.shape, jnp.float32)

    @pl.when(has_right)
    def _():
        for block in range(groups):
            behind(block).wait_recv()
            out_ref[block, pl.ds(LEFT + frames, RIGHT), :] = right_in[block]
            ahead(block).wait_send()

    @pl.when(me == total - 1)
    def _():
        out_ref[:, pl.ds(LEFT + frames, RIGHT), :] = jnp.zeros(right_in.shape, jnp.float32)


def similarities(queries, database, n_db, n_pb):
    rows, depth = queries.shape
    frames = database.shape[0]
    groups = n_pb // 2
    far = (max(groups - 1, 1), CHUNKS)
    dma = pltpu.SemaphoreType.DMA
    return pl.pallas_call(
        functools.partial(similarity_kernel, n_db, n_pb),
        out_shape=jax.ShapeDtypeStruct((groups, LEFT + frames + RIGHT, 2 * rows), jnp.float32),
        in_specs=[pl.BlockSpec(memory_space=pltpu.HBM)] * 2,
        out_specs=pl.BlockSpec(memory_space=pltpu.VMEM),
        scratch_shapes=[
            pltpu.VMEM((groups, 2 * rows, depth), jnp.bfloat16),
            pltpu.VMEM((frames, depth), jnp.bfloat16),
            pltpu.VMEM((groups, LEFT, 2 * rows), jnp.float32),
            pltpu.VMEM((groups, RIGHT, 2 * rows), jnp.float32),
            dma, dma, dma(far), dma(far), dma, dma, dma(far), dma(far),
            dma((2, *far)), dma((2, *far)), dma((2, groups)), dma((2, groups)),
        ],
        compiler_params=pltpu.CompilerParams(
            collective_id=0, has_side_effects=True, vmem_limit_bytes=60 * 1024 * 1024
        ),
    )(queries, database)


def score_kernel(band_total, n_pb, slopes_ref, sim_ref, out_ref, field, normed, two, four, eight, best):
    pieces, span, width = sim_ref.shape
    frames = out_ref.shape[1]
    anchor = (lax.axis_index("db") * n_pb + lax.axis_index("pb")) * frames - LEFT

    ids = lax.broadcasted_iota(jnp.int32, (span, width), 0) + anchor
    inside = jnp.logical_and(ids >= 0, ids < band_total)
    for p in range(pieces):
        field[p] = jnp.where(inside, sim_ref[p], 0.0)

    first, count = 8, span - 16
    center_ids = lax.broadcasted_iota(jnp.int32, (count, width), 0) + (anchor + first)
    counted = jnp.minimum(center_ids + RADIUS, band_total - 1) - jnp.maximum(center_ids - RADIUS, 0) + 1
    share = 1.0 / jnp.maximum(counted, 1).astype(jnp.float32)
    keep = jnp.logical_and(center_ids >= 0, center_ids < band_total)
    for p in range(pieces):
        first_sum = None
        for offset in range(-RADIUS, RADIUS + 1):
            part = field[p, pl.ds(first + offset, count), :]
            square = part * part
            first_sum = part if first_sum is None else first_sum + part
            second_sum = square if offset == -RADIUS else second_sum + square
        average = first_sum * share
        spread = second_sum * share - average * average
        center = field[p, pl.ds(first, count), :]
        value = (center - average) * lax.rsqrt(jnp.maximum(spread, variance_floor))
        normed[p, pl.ds(first, count), :] = jnp.where(keep, value, 0.0)

    lane = lax.broadcasted_iota(jnp.int32, (1, width), 1)

    def lagged(source, lo, steps, slope):
        rows = span - RIGHT - lo
        earlier, parts = 0.0, []
        for p in range(pieces):
            rolled = pltpu.roll(source[p, pl.ds(lo - steps * slope, rows), :], steps, 1)
            parts.append(jnp.where(lane < steps, earlier, rolled))
            earlier = rolled
        return parts

    best[...] = jnp.full(best.shape, -jnp.inf, jnp.float32)
    for slope in range(1, SMAX + 1):
        present = slopes_ref[0] == slope
        for index in range(1, slopes_ref.shape[0]):
            present = jnp.logical_or(present, slopes_ref[index] == slope)

        @pl.when(present)
        def _():
            for source, target, lo, steps in ((normed, two, 16, 1), (two, four, 32, 2), (four, eight, 80, 4)):
                parts = lagged(source, lo, steps, slope)
                for p in range(pieces):
                    target[p, pl.ds(lo, span - RIGHT - lo), :] = source[p, pl.ds(lo, span - RIGHT - lo), :] + parts[p]
            upper = lagged(eight, LEFT, 8, slope)
            tail = lagged(four, LEFT, 16, slope)
            for p in range(pieces):
                summed = eight[p, pl.ds(LEFT, frames), :] + upper[p] + tail[p]
                best[p] = jnp.maximum(best[p], summed)

    for p in range(pieces):
        out_ref[p * width : (p + 1) * width, :] = best[p].T * SEQ ** (-0.5)


def scores(similarity, slopes, band_total, n_pb):
    pieces, span, width = similarity.shape
    frames = span - LEFT - RIGHT
    return pl.pallas_call(
        functools.partial(score_kernel, band_total, n_pb),
        out_shape=jax.ShapeDtypeStruct((pieces * width, frames), jnp.float32),
        in_specs=[pl.BlockSpec(memory_space=pltpu.SMEM), pl.BlockSpec(memory_space=pltpu.VMEM)],
        out_specs=pl.BlockSpec(memory_space=pltpu.VMEM),
        scratch_shapes=[pltpu.VMEM((pieces, span, width), jnp.float32)] * 5
        + [pltpu.VMEM((pieces, frames, width), jnp.float32)],
        compiler_params=pltpu.CompilerParams(vmem_limit_bytes=48 * 1024 * 1024),
    )(slopes, similarity)


def on_device(n_db, n_pb, queries, database, slopes):
    similarity = similarities(queries, database, n_db, n_pb)
    return scores(similarity, slopes, database.shape[0] * n_db * n_pb, n_pb)


def solution(mesh):
    placed = (P("pb", None), P(("db", "pb"), None), P())
    sizes = (mesh.shape["db"], mesh.shape["pb"])
    return jax.shard_map(
        functools.partial(on_device, *sizes),
        mesh=mesh,
        in_specs=placed,
        out_specs=P(None, ("db", "pb")),
        check_vma=False,
    )
```

time: 26.7 us -> 27 us (1.011)
  the two profiles are of different devices: /device:TPU:8 before, /device:TPU:24 now
where the time goes in v3:
time: 27 us; the launch traced here: 26.9 us
  Pallas kernels  25.9 us (96%)
  local copies, waits for them, and re-layouts  1 us (4%)
    pallas_call x1, Pallas kernels, similarities(): pl.pallas_call(functools.partial(similarity_kernel, n_db, n_pb), out_shap...  21 us
    pallas_call x1, Pallas kernels, scores(): pl.pallas_call(functools.partial(score_kernel, band_total, n_pb), out_sha...  4.9 us
    unnamed x4, local copies, waits for them, and re-layouts  1 us

profile of v3, /device:TPU:24, one launch (start us, length us, event | category | flops | bytes accessed | tf_op | source)
XLA Modules:
  0.0 26.9 jit_solution(1250194351121050811)
XLA Ops:
  0.0 0.0 copy-start.1
  0.0 21.0 %shard_map.37.sim_ref = f32[2,392,128]{2,1,0:T(8,128)} custom-call(bf16[64,4096]{1,0:T(8,128)(2,1)} %q_ref.1, bf16[256,4096]{1,0:T(8,128)(2,1)} %base_ref.1), custom_call_target="tpu_custom_call" | custom-call | tf_op jit(solution)/shard_map/pallas_call | solution.py:215
  21.0 0.0 copy-done.1
  21.0 0.0 copy-start
  21.0 1.0 %copy-done = f32[2,392,128]{2,1,0:T(8,128)S(1)} copy-done((f32[2,392,128]{2,1,0:T(8,128)S(1)}, f32[2,392,128]{2,1,0:T(8,128)}, u32[]{:S(2)}) %copy-start) | copy-done | bytes 401432
  22.0 4.9 %shard_map.38 = f32[256,256]{1,0:T(8,128)} custom-call(s32[5]{0:T(128)S(1)} %copy-done.1, f32[2,392,128]{2,1,0:T(8,128)S(1)} %copy-done), custom_call_target="tpu_custom_call" | custom-call | tf_op jit(solution)/shard_map/pallas_call | solution.py:298
Async XLA Ops:
  0.0 21.0 %copy-start.1 = (s32[5]{0:T(128)S(1)}, s32[5]{0:T(128)}, u32[]{:S(2)}) copy-start(s32[5]{0:T(128)} %slopes_ref.1) | copy-start | bytes 64
  21.0 1.0 %copy-start = (f32[2,392,128]{2,1,0:T(8,128)S(1)}, f32[2,392,128]{2,1,0:T(8,128)}, u32[]{:S(2)}) copy-start(f32[2,392,128]{2,1,0:T(8,128)} %shard_map.37.sim_ref) | copy-start | bytes 1204228
